TPU v7x, 256 devices: a whole 4x4x8 slice. The times are simulated.
256 devices in a mesh: row: 8 (over y, core), col: 32 (over x, z).
Axes of the slice: x: 4, y: 4, z: 8, core: 2. Of those that a mesh axis runs over, the one named last changes fastest.
Arguments:
- adjoint: bfloat16 [16384, 16384], P('row', 'col'), may hold values from -1 to 1, as said below
- taper: int32 [64, 64], replicated, may hold values from 0 to 1, as said below
- panel_two: bfloat16 [16384, 1024], P(('row', 'col')), may hold values from -6 to 6
- panel_one: bfloat16 [16384, 1024], P(('row', 'col')), may hold values from -6 to 6
- incoming: float32 [16384, 1024], P('col', 'row'), may hold values from -6 to 6
- inverse_factor: bfloat16 [1024, 1024], P('row'), may hold values from -1 to 1, as said below
Outputs:
- second_grad: float32 [16384, 1024], P('col', 'row')
- first_grad: float32 [16384, 1024], P('col', 'row')
Inputs may be any that keep to these rules, and one draw needn't show every extreme that they name: `taper`: symmetric in its two indices; every entry with |a - b| <= 1 is 1. `adjoint`: symmetric. `inverse_factor`: lower triangular with a positive diagonal.
All inputs are finite; a program needn't handle non-finite values.
Results may differ from a plain program's by a relative error of at most 0.0025.
Values may be sent and summed in bfloat16 or wider, within the bound.
No kernel may reach another device: no remote copies, remote signals or barrier semaphores. Data moves between devices by JAX's collectives and lax.ppermute only.
A program may use at most 64 MiB of HBM per device.

v0:
```python
import jax
import jax.numpy as jnp
from jax import lax
from jax.sharding import PartitionSpec as P

BLK = 256


def broadcast(value, axis, source):
    kept = jnp.where(lax.axis_index(axis) == source, value, 0).astype(value.dtype)
    return lax.psum(kept, axis)


def mask_tiles(taper, row_tiles, col_tiles):
    first_row = lax.axis_index("row") * row_tiles
    first_col = lax.axis_index("col") * col_tiles
    return lax.dynamic_slice(taper, (first_row, first_col), (row_tiles, col_tiles))


def masked_local(adjoint, mask_block, tile_size):
    row_count, col_count = adjoint.shape
    shaped = adjoint.reshape(row_count // tile_size, tile_size, col_count // tile_size, tile_size)
    keep_mask = mask_block.astype(adjoint.dtype)[:, None, :, None]
    return (shaped * keep_mask).reshape(row_count, col_count)


def local(adjoint, taper, panel_two, panel_one, incoming, inverse_factor):
    tile_size = BLK
    row_tiles = adjoint.shape[0] // tile_size
    col_tiles = adjoint.shape[1] // tile_size
    mask_block = mask_tiles(taper, row_tiles, col_tiles)

    def gather_rows(panel):
        return lax.all_gather(panel, "col", axis=0, tiled=True)

    def spread(mirror_term):
        return lax.psum_scatter(mirror_term, "row", scatter_dimension=1, tiled=True)

    masked = masked_local(adjoint, mask_block, tile_size)

    def mirror(gathered):
        return lax.dot_general(
            masked, gathered, (((0,), (0,)), ((), ())), preferred_element_type=jnp.float32
        )

    rows_second = gather_rows(panel_two)
    second_grad = incoming + spread(-2.0 * mirror(rows_second))
    second_rounded = second_grad.astype(jnp.bfloat16)
    rows_first = gather_rows(panel_one)
    panel_width = panel_one.shape[1]
    diagonal_block = broadcast(rows_first[:panel_width], "row", 0)
    first_term = -2.0 * mirror(rows_first)
    partial_value = jnp.dot(second_rounded, inverse_factor, preferred_element_type=jnp.float32)
    carried = lax.psum(partial_value, "row")
    slab_rows = inverse_factor.shape[0]
    columns = lax.dynamic_slice_in_dim(
        diagonal_block, lax.axis_index("row") * slab_rows, slab_rows, 1
    ).astype(jnp.float32)
    carried_term = jnp.dot(
        carried, columns, precision=lax.Precision.HIGHEST, preferred_element_type=jnp.float32
    )
    first_grad = spread(first_term) - carried_term
    return (second_grad, first_grad)


def solution(mesh):
    in_specs = (
        P("row", "col"),
        P(),
        P(("row", "col"), None),
        P(("row", "col"), None),
        P("col", "row"),
        P("row", None),
    )
    out_specs = (P("col", "row"), P("col", "row"))
    return jax.shard_map(local, mesh=mesh, in_specs=in_specs, out_specs=out_specs, check_vma=False)
```

profile of v0, /device:TPU:2, one launch (start us, length us, event | category | flops | bytes accessed | tf_op | source)
XLA Modules:
  0.0 405.2 jit_solution(9717838235637787397)
XLA Ops:
  7.2 0.0 copy-start
  7.2 0.0 all-gather.3.cloned.1.call-start
  7.2 0.7 all-gather.3.cloned.1.call-update
  7.9 0.0 all-gather.5.cloned.1.call-start
  8.0 0.7 all-gather.5.cloned.1.call-update
  8.7 0.0 reduce-scatter.3.cloned.1.call-start
  8.7 0.8 dynamic-slice_convert_fusion
  9.5 1.1 mul.28
  10.6 0.5 copy.8
  11.1 82.9 %all-gather.3.cloned.1.call-done = bf16[2048,1024]{1,0:T(8,128)(2,1)} async-done(((bf16[64,1024]{1,0:T(8,128)(2,1)}), bf16[2048,1024]{1,0:T(8,128)(2,1)}) %all-gather.3.cloned.1.call-update) | async-done | bytes 4194320 | tf_op jit(solution)/shard_map/all_gather | solution.py:34
  94.1 6.5 %convolution_multiply_fusion.1 = f32[512,1024]{1,0:T(8,128)} fusion(bf16[2048,1024]{1,0:T(8,128)(2,1)} %all-gather.3.cloned.1.call-done, bf16[2048,512]{1,0:T(8,128)(2,1)} %param.6, bf16[2048,512]{1,0:T(8,128)(2,1)S(1)} %bitcast.8), kind=kOutput, calls=%fused_computation.2 | convolution fusion | flops 2149056512 | bytes 10485760 | tf_op jit(solution)/shard_map/dot_general | solution.py:42
  100.6 0.0 reduce-scatter.3.cloned.1.call-update
  100.6 0.0 all-reduce.5.cloned.1.call-start
  100.7 75.0 %all-gather.5.cloned.1.call-done = bf16[2048,1024]{1,0:T(8,128)(2,1)} async-done(((bf16[64,1024]{1,0:T(8,128)(2,1)}), bf16[2048,1024]{1,0:T(8,128)(2,1)}) %all-gather.5.cloned.1.call-update) | async-done | bytes 4194320 | tf_op jit(solution)/shard_map/all_gather | solution.py:34
  175.7 3.1 slice_select_fusion
  178.8 0.0 all-reduce.5.cloned.1.call-update
  178.8 0.0 reduce-scatter.5.cloned.1.call-start
  178.9 6.5 %convolution_multiply_fusion = f32[512,1024]{1,0:T(8,128)} fusion(bf16[2048,1024]{1,0:T(8,128)(2,1)} %all-gather.5.cloned.1.call-done, bf16[2048,512]{1,0:T(8,128)(2,1)} %param.6, bf16[2048,512]{1,0:T(8,128)(2,1)S(1)} %bitcast.9), kind=kOutput, calls=%fused_computation.1 | convolution fusion | flops 2149056512 | bytes 10485760 | tf_op jit(solution)/shard_map/dot_general | solution.py:42
  185.4 0.0 reduce-scatter.5.cloned.1.call-update
  185.4 0.0 all-reduce.3.cloned.1.call-start
  185.5 27.6 %reduce-scatter.3.cloned.1.call-done = f32[512,128]{1,0:T(8,128)} async-done(((f32[512,1024]{1,0:T(8,128)}), f32[512,128]{1,0:T(8,128)}) %reduce-scatter.3.cloned.1.call-update) | async-done | bytes 262160 | tf_op jit(solution)/shard_map/reduce_scatter | solution.py:37
  213.0 0.0 copy-done.2
  213.0 1.0 add.22
  214.0 0.0 copy-done
  214.0 0.0 copy-start.1
  214.0 1.8 fusion.3
  215.8 0.0 all-reduce.3.cloned.1.call-update
  215.8 0.0 copy-done.1
  215.8 69.0 %all-reduce.5.cloned.1.call-done = bf16[1024,1024]{1,0:T(8,128)(2,1)} async-done(((bf16[1024,1024]{1,0:T(8,128)(2,1)}), bf16[1024,1024]{1,0:T(8,128)(2,1)}) %all-reduce.5.cloned.1.call-update) | async-done | bytes 2097168 | tf_op jit(solution)/shard_map/psum | solution.py:11
  284.9 38.1 %reduce-scatter.5.cloned.1.call-done = f32[512,128]{1,0:T(8,128)} async-done(((f32[512,1024]{1,0:T(8,128)}), f32[512,128]{1,0:T(8,128)}) %reduce-scatter.5.cloned.1.call-update) | async-done | bytes 262160 | tf_op jit(solution)/shard_map/reduce_scatter | solution.py:37
  323.0 71.9 %all-reduce.3.cloned.1.call-done = f32[512,1024]{1,0:T(8,128)} async-done(((f32[512,1024]{1,0:T(8,128)}), f32[512,1024]{1,0:T(8,128)}) %all-reduce.3.cloned.1.call-update) | async-done | bytes 2097168 | tf_op jit(solution)/shard_map/psum | solution.py:54
  394.9 3.4 convolution_subtract_fusion
  (1 shorter events, 0.0 us)
Async XLA Ops:
  7.2 206.8 %copy-start = (bf16[128,1024]{1,0:T(8,128)(2,1)S(1)}, bf16[128,1024]{1,0:T(8,128)(2,1)}, u32[]{:S(2)}) copy-start(bf16[128,1024]{1,0:T(8,128)(2,1)} %param.11) | copy-start | bytes 786436
  7.2 86.9 %all-gather.3.cloned.1.call-start = ((), (), s32[]{:S(2)}) async-start(), calls=%async_computation.2 | async-start | bytes 4325376 | tf_op jit(solution)/shard_map/all_gather | solution.py:34
  7.9 167.8 %all-gather.5.cloned.1.call-start = ((), (), s32[]{:S(2)}) async-start(), calls=%async_computation.4 | async-start | bytes 4325376 | tf_op jit(solution)/shard_map/all_gather | solution.py:34
  8.7 204.4 %reduce-scatter.3.cloned.1.call-start = ((), (), s32[]{:S(2)}) async-start(), calls=%async_computation.3 | async-start | bytes 2359296 | tf_op jit(solution)/shard_map/reduce_scatter | solution.py:37
  100.6 184.2 %all-reduce.5.cloned.1.call-start = ((), (), s32[]{:S(2)}) async-start(), calls=%async_computation.7 | async-start | bytes 4194304 | tf_op jit(solution)/shard_map/psum | solution.py:11
  178.8 144.2 %reduce-scatter.5.cloned.1.call-start = ((), (), s32[]{:S(2)}) async-start(), calls=%async_computation.5 | async-start | bytes 2359296 | tf_op jit(solution)/shard_map/reduce_scatter | solution.py:37
  185.4 27.7 %copy-start.2 = (f32[512,128]{1,0:T(8,128)S(1)}, f32[512,128]{1,0:T(8,128)}, u32[]{:S(2)}) copy-start(f32[512,128]{1,0:T(8,128)} %param.10) | copy-start | bytes 786436
  185.4 209.5 %all-reduce.3.cloned.1.call-start = ((), (), s32[]{:S(2)}) async-start(), calls=%async_computation.6 | async-start | bytes 4194304 | tf_op jit(solution)/shard_map/psum | solution.py:54
  214.0 1.8 copy-start.1
Sparse Core Ops, SparseCore 0:
  10.6 83.4 all-gather.2
  96.7 78.9 all-gather.4
  178.3 34.7 reduce-scatter.2
  215.2 69.5 all-reduce.4
  287.3 35.6 reduce-scatter.4
  325.2 69.6 all-reduce.2
where the time goes:
time: 405 us
  waiting for transfers between devices  366 us (90%)
  matrix products  18.3 us (5%)
  between operations  14.2 us (4%)
  other arithmetic  4.82 us (1%)
    all_gather x2, waiting for transfers between devices, gather_rows(): return lax.all_gather(panel, 'col', axis=0, tiled=True)  158 us
    psum x1, waiting for transfers between devices, local(): carried = lax.psum(partial_value, 'row')  71.9 us
    psum x1, waiting for transfers between devices, broadcast(): return lax.psum(kept, axis)  69 us
    reduce_scatter x2, waiting for transfers between devices, spread(): return lax.psum_scatter(mirror_term, 'row', scatter_dimension=1, tiled=True)  65.7 us
    dot_general x2, matrix products, mirror(): lax.dot_general(masked, gathered, (((0,), (0,)), ((), ())), preferred_ele...  13.1 us
  transfers between devices with their start and end apart: 6, of which 6 were waited for; matrix products, arithmetic and copies ran while one was open for 5% of the time, Pallas kernels for 0%

commit v1 on v0

--- a/solution.py
+++ b/solution.py
@@ -51,7 +51,7 @@
     diagonal_block = broadcast(rows_first[:panel_width], "row", 0)
     first_term = -2.0 * mirror(rows_first)
     partial_value = jnp.dot(second_rounded, inverse_factor, preferred_element_type=jnp.float32)
-    carried = lax.psum(partial_value, "row")
+    carried = jnp.sum(lax.all_gather(partial_value, "row"), axis=0)
     slab_rows = inverse_factor.shape[0]
     columns = lax.dynamic_slice_in_dim(
         diagonal_block, lax.axis_index("row") * slab_rows, slab_rows, 1

time: 405 us -> 427 us (1.054)
  waiting for transfers between devices: 366 us -> 380 us
  other arithmetic: 4.82 us -> 12.8 us
    all_gather x0 -> x1, waiting for transfers between devices: none -> 78.1 us  [local(): carried = jnp.sum(lax.all_gather(partial_value, 'row'), axis=0)]
    psum x1 -> x0, waiting for transfers between devices: 71.9 us -> none  [local(): carried = lax.psum(partial_value, 'row')]
    reduce_sum x0 -> x1, other arithmetic: none -> 7.96 us  [local(): carried = jnp.sum(lax.all_gather(partial_value, 'row'), axis=0)]
    reduce_scatter x2, waiting for transfers between devices: 65.7 us -> 72.2 us  [spread(): return lax.psum_scatter(mirror_term, 'row', scatter_dimension=1, tiled=True)]
    all_gather x2, waiting for transfers between devices: 158 us -> 163 us  [gather_rows(): return lax.all_gather(panel, 'col', axis=0, tiled=True)]
where the time goes in v1:
time: 427 us
  waiting for transfers between devices  380 us (89%)
  matrix products  17.6 us (4%)
  between operations  14.2 us (3%)
  other arithmetic  12.8 us (3%)
    all_gather x2, waiting for transfers between devices, gather_rows(): return lax.all_gather(panel, 'col', axis=0, tiled=True)  163 us
    all_gather x1, waiting for transfers between devices, local(): carried = jnp.sum(lax.all_gather(partial_value, 'row'), axis=0)  78.1 us
    reduce_scatter x2, waiting for transfers between devices, spread(): return lax.psum_scatter(mirror_term, 'row', scatter_dimension=1, tiled=True)  72.2 us
    psum x1, waiting for transfers between devices, broadcast(): return lax.psum(kept, axis)  65.7 us
    dot_general x2, matrix products, mirror(): lax.dot_general(masked, gathered, (((0,), (0,)), ((), ())), preferred_ele...  13 us
  transfers between devices with their start and end apart: 6, of which 6 were waited for; matrix products, arithmetic and copies ran while one was open for 5% of the time, Pallas kernels for 0%

profile of v1, /device:TPU:2, one launch (start us, length us, event | category | flops | bytes accessed | tf_op | source)
XLA Modules:
  0.0 426.7 jit_solution(10190039708352052983)
XLA Ops:
  7.2 0.0 copy-start
  7.2 0.0 all-gather.5.cloned.1.call-start
  7.2 0.7 all-gather.5.cloned.1.call-update
  7.9 0.0 reduce-scatter.3.cloned.1.call-start
  8.0 0.8 dynamic-slice_convert_fusion
  8.7 1.1 mul.28
  9.9 0.5 copy.8
  10.4 83.7 %all-gather.5.cloned.1.call-done = bf16[2048,1024]{1,0:T(8,128)(2,1)} async-done(((bf16[64,1024]{1,0:T(8,128)(2,1)}), bf16[2048,1024]{1,0:T(8,128)(2,1)}) %all-gather.5.cloned.1.call-update) | async-done | bytes 4194320 | tf_op jit(solution)/shard_map/all_gather | solution.py:34
  94.1 6.5 %convolution_multiply_fusion.1 = f32[512,1024]{1,0:T(8,128)} fusion(bf16[2048,1024]{1,0:T(8,128)(2,1)} %all-gather.5.cloned.1.call-done, bf16[2048,512]{1,0:T(8,128)(2,1)} %param.6, bf16[2048,512]{1,0:T(8,128)(2,1)S(1)} %bitcast.10), kind=kOutput, calls=%fused_computation.2 | convolution fusion | flops 2149056512 | bytes 10485760 | tf_op jit(solution)/shard_map/dot_general | solution.py:42
  100.6 0.0 reduce-scatter.3.cloned.1.call-update
  100.6 0.0 all-gather.7.cloned.1.call-start
  100.7 0.7 all-gather.7.cloned.1.call-update
  101.3 0.0 all-gather.9.cloned.1.call-start
  101.4 34.1 %reduce-scatter.3.cloned.1.call-done = f32[512,128]{1,0:T(8,128)} async-done(((f32[512,1024]{1,0:T(8,128)}), f32[512,128]{1,0:T(8,128)}) %reduce-scatter.3.cloned.1.call-update) | async-done | bytes 262160 | tf_op jit(solution)/shard_map/reduce_scatter | solution.py:37
  135.5 0.0 copy-done.2
  135.5 1.0 add.20
  136.5 0.0 copy-done
  136.5 0.0 copy-start.1
  136.5 1.8 fusion.3
  138.3 0.0 all-gather.9.cloned.1.call-update
  138.3 0.0 all-reduce.2.cloned.1.call-start
  138.4 79.0 %all-gather.7.cloned.1.call-done = bf16[2048,1024]{1,0:T(8,128)(2,1)} async-done(((bf16[64,1024]{1,0:T(8,128)(2,1)}), bf16[2048,1024]{1,0:T(8,128)(2,1)}) %all-gather.7.cloned.1.call-update) | async-done | bytes 4194320 | tf_op jit(solution)/shard_map/all_gather | solution.py:34
  217.4 3.1 slice_select_fusion
  220.5 0.0 all-reduce.2.cloned.1.call-update
  220.5 0.0 reduce-scatter.5.cloned.1.call-start
  220.6 6.5 %convolution_multiply_fusion = f32[512,1024]{1,0:T(8,128)} fusion(bf16[2048,1024]{1,0:T(8,128)(2,1)} %all-gather.7.cloned.1.call-done, bf16[2048,512]{1,0:T(8,128)(2,1)} %param.6, bf16[2048,512]{1,0:T(8,128)(2,1)S(1)} %bitcast.11), kind=kOutput, calls=%fused_computation.1 | convolution fusion | flops 2149056512 | bytes 10485760 | tf_op jit(solution)/shard_map/dot_general | solution.py:42
  227.1 0.0 reduce-scatter.5.cloned.1.call-update
  227.1 78.1 %all-gather.9.cloned.1.call-done = f32[4096,1024]{1,0:T(8,128)} async-done(((f32[512,1024]{1,0:T(8,128)}), f32[4096,1024]{1,0:T(8,128)}) %all-gather.9.cloned.1.call-update) | async-done | bytes 16777232 | tf_op jit(solution)/shard_map/all_gather | solution.py:54
  305.2 8.0 %reduce_sum.9 = f32[512,1024]{1,0:T(8,128)S(1)} reduce(f32[8,512,1024]{2,1,0:T(8,128)} %bitcast.8, f32[]{:T(128)} %constant.23.clone.1), dimensions={0}, to_apply=%region_2.3 | reduce | flops 3670016 | bytes 18874372 | tf_op jit(solution)/shard_map/reduce_sum | solution.py:54
  313.2 65.7 %all-reduce.2.cloned.1.call-done = bf16[1024,1024]{1,0:T(8,128)(2,1)} async-done(((bf16[1024,1024]{1,0:T(8,128)(2,1)}), bf16[1024,1024]{1,0:T(8,128)(2,1)}) %all-reduce.2.cloned.1.call-update) | async-done | bytes 2097168 | tf_op jit(solution)/shard_map/psum | solution.py:11
  378.9 38.1 %reduce-scatter.5.cloned.1.call-done = f32[512,128]{1,0:T(8,128)} async-done(((f32[512,1024]{1,0:T(8,128)}), f32[512,128]{1,0:T(8,128)}) %reduce-scatter.5.cloned.1.call-update) | async-done | bytes 262160 | tf_op jit(solution)/shard_map/reduce_scatter | solution.py:37
  417.0 2.8 convolution_subtract_fusion
  (2 shorter events, 0.0 us)
Async XLA Ops:
  7.2 129.3 %copy-start = (bf16[128,1024]{1,0:T(8,128)(2,1)S(1)}, bf16[128,1024]{1,0:T(8,128)(2,1)}, u32[]{:S(2)}) copy-start(bf16[128,1024]{1,0:T(8,128)(2,1)} %param.11) | copy-start | bytes 786436
  7.2 86.9 %all-gather.5.cloned.1.call-start = ((), (), s32[]{:S(2)}) async-start(), calls=%async_computation.2 | async-start | bytes 4325376 | tf_op jit(solution)/shard_map/all_gather | solution.py:34
  7.9 127.6 %reduce-scatter.3.cloned.1.call-start = ((), (), s32[]{:S(2)}) async-start(), calls=%async_computation.3 | async-start | bytes 2359296 | tf_op jit(solution)/shard_map/reduce_scatter | solution.py:37
  100.6 34.9 %copy-start.2 = (f32[512,128]{1,0:T(8,128)S(1)}, f32[512,128]{1,0:T(8,128)}, u32[]{:S(2)}) copy-start(f32[512,128]{1,0:T(8,128)} %param.10) | copy-start | bytes 786436
  100.6 116.8 %all-gather.7.cloned.1.call-start = ((), (), s32[]{:S(2)}) async-start(), calls=%async_computation.4 | async-start | bytes 4325376 | tf_op jit(solution)/shard_map/all_gather | solution.py:34
  101.3 203.9 %all-gather.9.cloned.1.call-start = ((), (), s32[]{:S(2)}) async-start(), calls=%async_computation.7 | async-start | bytes 18874368 | tf_op jit(solution)/shard_map/all_gather | solution.py:54
  136.5 1.8 copy-start.1
  138.3 240.6 %all-reduce.2.cloned.1.call-start = ((), (), s32[]{:S(2)}) async-start(), calls=%async_computation.6 | async-start | bytes 4194304 | tf_op jit(solution)/shard_map/psum | solution.py:11
  220.5 196.5 %reduce-scatter.5.cloned.1.call-start = ((), (), s32[]{:S(2)}) async-start(), calls=%async_computation.5 | async-start | bytes 2359296 | tf_op jit(solution)/shard_map/reduce_scatter | solution.py:37
Sparse Core Ops, SparseCore 0:
  10.6 83.4 all-gather.4
  100.7 34.7 reduce-scatter.2
  138.1 79.2 all-gather.6
  219.1 86.0 all-gather.8
  307.4 71.4 all-reduce.1
  381.3 35.6 reduce-scatter.4
